TPU v7x, 32 devices: a whole 2x2x4 slice. The times are simulated.
32 devices in a mesh: ctx: 8 (over z, y), tp: 4 (over x, core).
Axes of the slice: x: 2, y: 2, z: 4, core: 2. Of those that a mesh axis runs over, the one named last changes fastest.
Arguments:
- layer_inputs: bfloat16 [1536, 2048], P('ctx', 'tp'), may hold values from -6 to 6
- states: float32 [1536, 2048], P('ctx', 'tp'), may hold values from -0.7 to 0.7
- cotangent: float32 [1536, 2048], P('ctx', 'tp'), may hold values from -0.009765625 to 0.009765625
- block_weights: float32 [32, 64, 64], P('tp'), may hold values from -1 to 1
Outputs:
- grad_proj: float32 [2048, 2048], P(('ctx', 'tp'))
All inputs are finite; a program needn't handle non-finite values.
Results may differ from a plain program's by a relative error of at most 0.0029.
Values may be sent and summed in bfloat16 or wider, within the bound.
A program may use at most 64 MiB of HBM per device.

v0:
```python
import jax
import jax.numpy as jnp
from jax import lax
from jax.sharding import PartitionSpec as P

exact = lax.Precision.HIGHEST


def from_behind(value, axis, by):
    size = lax.axis_size(axis)
    pairs = [(i, i + by) for i in range(size) if 0 <= i + by < size]
    return lax.ppermute(value, axis, pairs)


def compose(right_map, left_map):
    right_mat, right_vec = right_map
    left_mat, left_vec = left_map
    joined = jnp.einsum("hisj,hjsk->hisk", left_mat, right_mat, precision=exact)
    shifted = left_vec + jnp.einsum("hisj,hjs->his", left_mat, right_vec, precision=exact)
    return (joined, shifted)


def on_device(layer_inputs, states, cotangent, block_weights):
    tokens_here = states.shape[0]
    head_local = block_weights.shape[0]
    head_width = block_weights.shape[1]
    block_len = 32
    blocks = tokens_here // block_len

    def arrange(values):
        shaped = values.reshape(blocks, block_len, head_local, head_width)
        return jnp.transpose(shaped, (1, 2, 3, 0))

    slopes = arrange(1.0 - states * states)
    upstream = arrange(cotangent)

    def build_step(affine_maps, pieces):
        matrices, offsets = affine_maps
        slope_now, grad_now = pieces
        pulled = jnp.einsum("hji,hjsk->hisk", block_weights, matrices, precision=exact)
        matrices = slope_now[..., None] * pulled
        offsets = slope_now * (
            grad_now + jnp.einsum("hji,hjs->his", block_weights, offsets, precision=exact)
        )
        return ((matrices, offsets), None)

    identity_mats = jnp.broadcast_to(
        jnp.eye(head_width, dtype=jnp.float32)[None, :, None, :],
        (head_local, head_width, blocks, head_width),
    )
    zero_offsets = jnp.zeros((head_local, head_width, blocks), jnp.float32)
    (matrices, offsets), unused = lax.scan(
        build_step, (identity_mats, zero_offsets), (slopes, upstream), reverse=True
    )
    flipped = (jnp.flip(matrices, 2), jnp.flip(offsets, 2))
    suffix = lax.associative_scan(compose, flipped, axis=2)
    suffix_mat = jnp.flip(suffix[0], 2)
    suffix_vec = jnp.flip(suffix[1], 2)
    device_mat = suffix_mat[:, :, :1, :]
    device_vec = suffix_vec[:, :, :1]

    def relay_turn(step_index, entering):
        leaving = device_vec + jnp.einsum("hisj,hjs->his", device_mat, entering, precision=exact)
        return from_behind(leaving, "ctx", -1)

    entering = lax.fori_loop(0, lax.axis_size("ctx") - 1, relay_turn, jnp.zeros_like(device_vec))
    later_mat = suffix_mat[:, :, 1:, :]
    later_vector = suffix_vec[:, :, 1:]
    inner_starts = later_vector + jnp.einsum(
        "hisj,hj->his", later_mat, entering[:, :, 0], precision=exact
    )
    starts = jnp.concatenate([inner_starts, entering], axis=2)

    def solve_step(subsequent_step, pieces):
        slope_now, grad_now = pieces
        current = slope_now * (
            grad_now + jnp.einsum("hji,hjs->his", block_weights, subsequent_step, precision=exact)
        )
        return (current, current)

    remaining_part, adjoints = lax.scan(solve_step, starts, (slopes, upstream), reverse=True)
    adjoint_bf = (
        jnp.transpose(adjoints, (1, 2, 3, 0))
        .reshape(head_local * head_width, tokens_here)
        .astype(jnp.bfloat16)
    )
    gathered = lax.all_gather(layer_inputs, "tp", axis=1, tiled=True)
    summed = lax.psum_scatter(
        lax.dot_general(
            gathered, adjoint_bf, (((0,), (1,)), ((), ())), preferred_element_type=jnp.float32
        ),
        "ctx",
        scatter_dimension=0,
        tiled=True,
    )
    result = lax.all_to_all(summed, "tp", split_axis=0, concat_axis=1, tiled=True)
    return result


def solution(mesh):
    in_specs = (P("ctx", "tp"), P("ctx", "tp"), P("ctx", "tp"), P("tp", None, None))
    out_specs = P(("ctx", "tp"), None)
    return jax.shard_map(
        on_device, mesh=mesh, in_specs=in_specs, out_specs=out_specs, check_vma=False
    )
```

profile of v0, /device:TPU:0, one launch (start us, length us, event | category | flops | bytes accessed | tf_op | source)
XLA Modules:
  0.0 375.9 jit_solution(12649809995185188845)
XLA Ops:
  11.1 115.7 %while.45 = (s32[]{:T(128)}, f32[8,64,6,64]{3,1,2,0:T(8,128)S(1)}, f32[8,64,6]{1,2,0:T(8,128)S(1)}, f32[32,8,64,6]{2,3,1,0:T(8,128)}, f32[8,64,64]{2,1,0:T(8,128...) while((s32[]{:T(128)}, f32[8,64,6,64]{3,1,2,0:T(8,128)S(1)}, ...), condition=%wide.region_1.2_spmd.clone, body=%wide.region_0.1_spmd.clone.sunk | while | flops 153560064 | bytes 3518595 | solution.py:52
  12.0 1.5 convolution_multiply_fusion.2
  15.7 1.5 convolution_multiply_fusion.2
  19.3 1.5 convolution_multiply_fusion.2
  22.9 1.5 convolution_multiply_fusion.2
  26.5 1.5 convolution_multiply_fusion.2
  30.1 1.5 convolution_multiply_fusion.2
  33.7 1.5 convolution_multiply_fusion.2
  37.3 1.5 convolution_multiply_fusion.2
  41.0 1.5 convolution_multiply_fusion.2
  44.6 1.5 convolution_multiply_fusion.2
  51.8 1.5 convolution_multiply_fusion.2
  55.4 1.5 convolution_multiply_fusion.2
  59.0 1.5 convolution_multiply_fusion.2
  62.7 1.5 convolution_multiply_fusion.2
  66.3 1.5 convolution_multiply_fusion.2
  69.9 1.5 convolution_multiply_fusion.2
  73.5 1.5 convolution_multiply_fusion.2
  77.1 1.5 convolution_multiply_fusion.2
  80.7 1.5 convolution_multiply_fusion.2
  84.4 1.5 convolution_multiply_fusion.2
  88.0 1.5 convolution_multiply_fusion.2
  91.6 1.5 convolution_multiply_fusion.2
  95.2 1.5 convolution_multiply_fusion.2
  98.8 1.5 convolution_multiply_fusion.2
  102.4 1.5 convolution_multiply_fusion.2
  106.1 1.5 convolution_multiply_fusion.2
  113.3 1.5 convolution_multiply_fusion.2
  124.1 1.5 convolution_multiply_fusion.2
  132.9 8.5 %pad.66 = f32[8,64,5,64]{1,3,2,0:T(8,128)} pad(f32[8,64,3,64]{1,3,2,0:T(8,128)S(1)} %pad_add_fusion, f32[]{:T(128)} %constant.84.clone.1), padding=0_0_0x0_0_0x0_0_1x0_0_0 | pad | bytes 1048580
  141.4 8.6 %pad.33 = f32[8,64,6,64]{1,3,2,0:T(8,128)} pad(f32[8,64,3,64]{1,3,2,0:T(8,128)S(1)} %pad_add_fusion, f32[]{:T(128)} %constant.84.clone.1), padding=0_0_0x0_0_0x1_0_1x0_0_0 | pad | bytes 1179652 | tf_op jit(solution)/shard_map/pad | solution.py:56
  150.0 1.8 convolution_bitcast_fusion.2
  151.7 1.6 copy.30
  155.7 8.5 %pad.32 = f32[8,64,6,64]{1,3,2,0:T(8,128)} pad(f32[8,64,3,64]{1,3,2,0:T(8,128)S(1)} %pad_maximum_fusion, f32[]{:T(128)} %constant.84.clone.1), padding=0_0_0x0_0_0x0_1_1x0_0_0 | pad | bytes 1179652 | tf_op jit(solution)/shard_map/pad | solution.py:56
  165.9 48.5 %while.43 = (s32[]{:T(128)}, f32[8,64,1]{1,0,2:T(8,128)S(1)}, f32[8,64,1]{1,2,0:T(1,128)S(1)}, f32[8,64,1,64]{3,2,1,0:T(1,128)S(1)}, s32[]{:T(128)}) while((s32[]{:T(128)}, f32[8,64,1]{1,0,2:T(8,128)S(1)}, f32[8,64,1]{1,2,0:T(1,128)S(1)}, f32[8,64,1,64]{3,2,1,0:T(1,128)S(1)}, s32[]{:T(128)}) %tuple.93), condition=%wide.region_3.4_spmd, body=%wide.region_2.3_spmd.sunk | while | flops 393730 | bytes 149605 | solution.py:66
  167.8 5.2 %collective-permute-done = f32[8,64,1]{1,0,2:T(8,128)S(1)} collective-permute-done((f32[8,64,1]{1,0,2:T(8,128)S(1)}, f32[8,64,1]{1,0,2:T(8,128)S(1)}, u32[]{:S(2)}, u32[]{:S(2)}) %collective-permute-start) | collective-permute-done | bytes 2080 | tf_op jit(solution)/shard_map/while/body/eval_jaxpr/ppermute | solution.py:12
  174.8 5.1 %collective-permute-done = f32[8,64,1]{1,0,2:T(8,128)S(1)} collective-permute-done((f32[8,64,1]{1,0,2:T(8,128)S(1)}, f32[8,64,1]{1,0,2:T(8,128)S(1)}, u32[]{:S(2)}, u32[]{:S(2)}) %collective-permute-start) | collective-permute-done | bytes 2080 | tf_op jit(solution)/shard_map/while/body/eval_jaxpr/ppermute | solution.py:12
  181.7 5.1 %collective-permute-done = f32[8,64,1]{1,0,2:T(8,128)S(1)} collective-permute-done((f32[8,64,1]{1,0,2:T(8,128)S(1)}, f32[8,64,1]{1,0,2:T(8,128)S(1)}, u32[]{:S(2)}, u32[]{:S(2)}) %collective-permute-start) | collective-permute-done | bytes 2080 | tf_op jit(solution)/shard_map/while/body/eval_jaxpr/ppermute | solution.py:12
  188.6 5.1 %collective-permute-done = f32[8,64,1]{1,0,2:T(8,128)S(1)} collective-permute-done((f32[8,64,1]{1,0,2:T(8,128)S(1)}, f32[8,64,1]{1,0,2:T(8,128)S(1)}, u32[]{:S(2)}, u32[]{:S(2)}) %collective-permute-start) | collective-permute-done | bytes 2080 | tf_op jit(solution)/shard_map/while/body/eval_jaxpr/ppermute | solution.py:12
  195.5 5.1 %collective-permute-done = f32[8,64,1]{1,0,2:T(8,128)S(1)} collective-permute-done((f32[8,64,1]{1,0,2:T(8,128)S(1)}, f32[8,64,1]{1,0,2:T(8,128)S(1)}, u32[]{:S(2)}, u32[]{:S(2)}) %collective-permute-start) | collective-permute-done | bytes 2080 | tf_op jit(solution)/shard_map/while/body/eval_jaxpr/ppermute | solution.py:12
  202.4 5.1 %collective-permute-done = f32[8,64,1]{1,0,2:T(8,128)S(1)} collective-permute-done((f32[8,64,1]{1,0,2:T(8,128)S(1)}, f32[8,64,1]{1,0,2:T(8,128)S(1)}, u32[]{:S(2)}, u32[]{:S(2)}) %collective-permute-start) | collective-permute-done | bytes 2080 | tf_op jit(solution)/shard_map/while/body/eval_jaxpr/ppermute | solution.py:12
  209.4 5.1 %collective-permute-done = f32[8,64,1]{1,0,2:T(8,128)S(1)} collective-permute-done((f32[8,64,1]{1,0,2:T(8,128)S(1)}, f32[8,64,1]{1,0,2:T(8,128)S(1)}, u32[]{:S(2)}, u32[]{:S(2)}) %collective-permute-start) | collective-permute-done | bytes 2080 | tf_op jit(solution)/shard_map/while/body/eval_jaxpr/ppermute | solution.py:12
  214.5 2.2 fusion.24
  217.5 37.3 %while.44 = (s32[]{:T(128)}, f32[8,64,6]{1,2,0:T(8,128)S(1)}, bf16[32,8,64,6]{2,3,1,0:T(8,128)(2,1)S(1)}, f32[32,8,64,6]{2,3,1,0:T(8,128)}, f32[32,8,64,6]{2,3,1...) while((s32[]{:T(128)}, f32[8,64,6]{1,2,0:T(8,128)S(1)}, ...), condition=%wide.region_5.6_spmd, body=%wide.region_4.5_spmd.sunk | while | flops 2365443 | bytes 409709 | solution.py:81
  255.1 8.6 %all_gather.3 = bf16[192,2048]{1,0:T(8,128)(2,1)S(1)} all-gather(bf16[192,512]{1,0:T(8,128)(2,1)S(1)} %copy-done.4), channel_id=1, replica_groups=mesh['ctx'=8,'tp'=4] {'tp'}, dimensions={1}, use_global_device_ids=true | all-gather | bytes 983040 | tf_op jit(solution)/shard_map/all_gather | solution.py:87
  263.7 2.7 convolution_bitcast_fusion
  266.5 89.2 %reduce-scatter.2.cloned.1.call-done = f32[256,512]{0,1:T(8,128)} async-done(((f32[2048,512]{0,1:T(8,128)}), f32[256,512]{0,1:T(8,128)}) %reduce-scatter.2.cloned.1.call-update) | async-done | bytes 524304 | tf_op jit(solution)/shard_map/reduce_scatter | solution.py:88
  356.9 11.4 %all_to_all.19 = f32[4,64,512]{2,1,0:T(8,128)S(1)} all-to-all(f32[4,64,512]{2,1,0:T(8,128)S(1)} %bitcast.157), channel_id=1, replica_groups=mesh['ctx'=8,'tp'=4] {'tp'}, dimensions={0} | all-to-all | bytes 1048576 | tf_op jit(solution)/shard_map/all_to_all | solution.py:96
  (288 shorter events, 138.8 us)
Async XLA Ops:
  6.5 349.1 %reduce-scatter.2.cloned.1.call-start = ((), (), s32[]{:S(2)}) async-start(), calls=%async_computation.2 | async-start | bytes 4718592 | tf_op jit(solution)/shard_map/reduce_scatter | solution.py:88
  7.6 1.7 copy-start.3
  9.4 1.6 copy-start
  130.6 1.1 copy-start.2
  151.7 1.6 slice-start.1
  153.4 1.3 slice-start
  155.7 8.5 %copy-start.1 = (f32[8,64,6,64]{1,3,2,0:T(8,128)S(1)}, f32[8,64,6,64]{1,3,2,0:T(8,128)}, u32[]{:S(2)}) copy-start(f32[8,64,6,64]{1,3,2,0:T(8,128)} %pad.33) | copy-start | bytes 2359300
  166.5 6.5 %collective-permute-start = (f32[8,64,1]{1,0,2:T(8,128)S(1)}, f32[8,64,1]{1,0,2:T(8,128)S(1)}, u32[]{:S(2)}, u32[]{:S(2)}) collective-permute-start(f32[8,64,1]{1,0,2:T(8,128)S(1)} %add_bitcast_fusion.2), channel_id=1, source_target_pairs={{4,0},{8,4},{12,8},{16,12},{20,16},{24,20},{28,24},{5,1},{9,5},{13... | collective-permute-start | bytes 6152 | tf_op jit(solution)/shard_map/while/body/eval_jaxpr/ppermute | solution.py:12
  173.4 6.4 %collective-permute-start = (f32[8,64,1]{1,0,2:T(8,128)S(1)}, f32[8,64,1]{1,0,2:T(8,128)S(1)}, u32[]{:S(2)}, u32[]{:S(2)}) collective-permute-start(f32[8,64,1]{1,0,2:T(8,128)S(1)} %add_bitcast_fusion.2), channel_id=1, source_target_pairs={{4,0},{8,4},{12,8},{16,12},{20,16},{24,20},{28,24},{5,1},{9,5},{13... | collective-permute-start | bytes 6152 | tf_op jit(solution)/shard_map/while/body/eval_jaxpr/ppermute | solution.py:12
  180.4 6.4 %collective-permute-start = (f32[8,64,1]{1,0,2:T(8,128)S(1)}, f32[8,64,1]{1,0,2:T(8,128)S(1)}, u32[]{:S(2)}, u32[]{:S(2)}) collective-permute-start(f32[8,64,1]{1,0,2:T(8,128)S(1)} %add_bitcast_fusion.2), channel_id=1, source_target_pairs={{4,0},{8,4},{12,8},{16,12},{20,16},{24,20},{28,24},{5,1},{9,5},{13... | collective-permute-start | bytes 6152 | tf_op jit(solution)/shard_map/while/body/eval_jaxpr/ppermute | solution.py:12
  187.3 6.4 %collective-permute-start = (f32[8,64,1]{1,0,2:T(8,128)S(1)}, f32[8,64,1]{1,0,2:T(8,128)S(1)}, u32[]{:S(2)}, u32[]{:S(2)}) collective-permute-start(f32[8,64,1]{1,0,2:T(8,128)S(1)} %add_bitcast_fusion.2), channel_id=1, source_target_pairs={{4,0},{8,4},{12,8},{16,12},{20,16},{24,20},{28,24},{5,1},{9,5},{13... | collective-permute-start | bytes 6152 | tf_op jit(solution)/shard_map/while/body/eval_jaxpr/ppermute | solution.py:12
  194.2 6.4 %collective-permute-start = (f32[8,64,1]{1,0,2:T(8,128)S(1)}, f32[8,64,1]{1,0,2:T(8,128)S(1)}, u32[]{:S(2)}, u32[]{:S(2)}) collective-permute-start(f32[8,64,1]{1,0,2:T(8,128)S(1)} %add_bitcast_fusion.2), channel_id=1, source_target_pairs={{4,0},{8,4},{12,8},{16,12},{20,16},{24,20},{28,24},{5,1},{9,5},{13... | collective-permute-start | bytes 6152 | tf_op jit(solution)/shard_map/while/body/eval_jaxpr/ppermute | solution.py:12
  201.1 6.4 %collective-permute-start = (f32[8,64,1]{1,0,2:T(8,128)S(1)}, f32[8,64,1]{1,0,2:T(8,128)S(1)}, u32[]{:S(2)}, u32[]{:S(2)}) collective-permute-start(f32[8,64,1]{1,0,2:T(8,128)S(1)} %add_bitcast_fusion.2), channel_id=1, source_target_pairs={{4,0},{8,4},{12,8},{16,12},{20,16},{24,20},{28,24},{5,1},{9,5},{13... | collective-permute-start | bytes 6152 | tf_op jit(solution)/shard_map/while/body/eval_jaxpr/ppermute | solution.py:12
  208.1 6.4 %collective-permute-start = (f32[8,64,1]{1,0,2:T(8,128)S(1)}, f32[8,64,1]{1,0,2:T(8,128)S(1)}, u32[]{:S(2)}, u32[]{:S(2)}) collective-permute-start(f32[8,64,1]{1,0,2:T(8,128)S(1)} %add_bitcast_fusion.2), channel_id=1, source_target_pairs={{4,0},{8,4},{12,8},{16,12},{20,16},{24,20},{28,24},{5,1},{9,5},{13... | collective-permute-start | bytes 6152 | tf_op jit(solution)/shard_map/while/body/eval_jaxpr/ppermute | solution.py:12
  217.5 37.6 %copy-start.4 = (bf16[192,512]{1,0:T(8,128)(2,1)S(1)}, bf16[192,512]{1,0:T(8,128)(2,1)}, u32[]{:S(2)}) copy-start(bf16[192,512]{1,0:T(8,128)(2,1)} %param.10) | copy-start | bytes 589828
Sparse Core Ops, SparseCore 0:
  266.6 88.9 reduce-scatter.1
where the time goes:
time: 383 us; the launch traced here: 376 us
  matrix products  136 us (36%)
  waiting for transfers between devices  125 us (33%)
  local copies, waits for them, and re-layouts  65 us (17%)
  blocking collectives  20 us (5%)
  between operations  13.7 us (4%)
  starting transfers between devices  9.06 us (2%)
  other arithmetic  4.9 us (1%)
    reduce_scatter x1, waiting for transfers between devices, on_device(): lax.psum_scatter(lax.dot_general(gathered, adjoint_bf, (((0,), (1,)), (()...  89.2 us
    dot_general x32, matrix products, build_step(): jnp.einsum('hji,hjsk->hisk', block_weights, matrices, precision=exact)  48.4 us
    dot_general x32, matrix products, solve_step(): jnp.einsum('hji,hjs->his', block_weights, subsequent_step, precision=exact)  36.3 us
    dot_general x32, matrix products, build_step(): jnp.einsum('hji,hjs->his', block_weights, offsets, precision=exact)  36.1 us
    ppermute x7, waiting for transfers between devices, from_behind(): return lax.ppermute(value, axis, pairs)  35.7 us
    mul x32, local copies, waits for them, and re-layouts, build_step(): matrices = slope_now[..., None] * pulled  24.5 us
    pad x6, local copies, waits for them, and re-layouts, on_device(): suffix = lax.associative_scan(compose, flipped, axis=2)  17.5 us
    unnamed x14, local copies, waits for them, and re-layouts  11.5 us
  transfers between devices with their start and end apart: 8, of which 8 were waited for; matrix products, arithmetic and copies ran while one was open for 0% of the time, Pallas kernels for 0%

commit v1 on v0

--- a/solution.py
+++ b/solution.py
@@ -4,6 +4,24 @@
 from jax.sharding import PartitionSpec as P
 
 exact = lax.Precision.HIGHEST
+
+
+def gather_around(value, axis, dim):
+    ways, here, turn = (lax.axis_size(axis), lax.axis_index(axis), value.shape[dim])
+    lengths = [n * ways if d == dim else n for d, n in enumerate(value.shape)]
+    full = lax.dynamic_update_slice_in_dim(
+        jnp.zeros(lengths, value.dtype), value, here * turn, axis=dim
+    )
+    going_up = going_down = value
+    for far in range(1, ways // 2 + 1):
+        going_up = lax.ppermute(going_up, axis, [(d, (d + 1) % ways) for d in range(ways)])
+        full = lax.dynamic_update_slice_in_dim(full, going_up, (here - far) % ways * turn, axis=dim)
+        if 2 * far < ways:
+            going_down = lax.ppermute(going_down, axis, [(d, (d - 1) % ways) for d in range(ways)])
+            full = lax.dynamic_update_slice_in_dim(
+                full, going_down, (here + far) % ways * turn, axis=dim
+            )
+    return full
 
 
 def from_behind(value, axis, by):
@@ -84,7 +102,7 @@
         .reshape(head_local * head_width, tokens_here)
         .astype(jnp.bfloat16)
     )
-    gathered = lax.all_gather(layer_inputs, "tp", axis=1, tiled=True)
+    gathered = gather_around(layer_inputs, "tp", 1)
     summed = lax.psum_scatter(
         lax.dot_general(
             gathered, adjoint_bf, (((0,), (1,)), ((), ())), preferred_element_type=jnp.float32

time: 383 us -> 354 us (0.924)
  local copies, waits for them, and re-layouts: 65 us -> 40.2 us
  blocking collectives: 20 us -> 12.3 us
    mul x32, local copies, waits for them, and re-layouts: 24.5 us -> 0.24 us  [build_step(): matrices = slope_now[..., None] * pulled]
    all_gather x1 -> x0, blocking collectives: 8.6 us -> none  [on_device(): gathered = lax.all_gather(layer_inputs, 'tp', axis=1, tiled=True)]
    unnamed x14 -> x16, local copies, waits for them, and re-layouts: 11.5 us -> 12.2 us
  transfers between devices with their start and end apart: 8 -> 11, of which waited for: 8 -> 9; matrix products, arithmetic and copies ran while one was open for 0% -> 51% of each run, Pallas kernels for 0% -> 0%
where the time goes in v1:
time: 354 us; the launch traced here: 349 us
  matrix products  136 us (38%)
  waiting for transfers between devices  127 us (36%)
  local copies, waits for them, and re-layouts  40.2 us (11%)
  between operations  13.9 us (4%)
  blocking collectives  12.3 us (3%)
  starting transfers between devices  11.5 us (3%)
  other arithmetic  4.91 us (1%)
    reduce_scatter x1, waiting for transfers between devices, on_device(): lax.psum_scatter(lax.dot_general(gathered, adjoint_bf, (((0,), (1,)), (()...  89.4 us
    dot_general x32, matrix products, build_step(): jnp.einsum('hji,hjsk->hisk', block_weights, matrices, precision=exact)  49.1 us
    dot_general x32, matrix products, solve_step(): jnp.einsum('hji,hjs->his', block_weights, subsequent_step, precision=exact)  36.2 us
    dot_general x32, matrix products, build_step(): jnp.einsum('hji,hjs->his', block_weights, offsets, precision=exact)  35.6 us
    ppermute x7, waiting for transfers between devices, from_behind(): return lax.ppermute(value, axis, pairs)  34.3 us
    pad x6, local copies, waits for them, and re-layouts, on_device(): suffix = lax.associative_scan(compose, flipped, axis=2)  17.5 us
    all_to_all x1, blocking collectives, on_device(): lax.all_to_all(summed, 'tp', split_axis=0, concat_axis=1, tiled=True)  12.3 us
    unnamed x16, local copies, waits for them, and re-layouts  12.2 us
  transfers between devices with their start and end apart: 11, of which 9 were waited for; matrix products, arithmetic and copies ran while one was open for 51% of the time, Pallas kernels for 0%

profile of v1, /device:TPU:0, one launch (start us, length us, event | category | flops | bytes accessed | tf_op | source)
XLA Modules:
  0.0 348.5 jit_solution(13701894190722713472)
XLA Ops:
  6.5 2.4 collective-permute-start.2
  12.9 89.9 %while.45 = (s32[]{:T(128)}, f32[8,64,6,64]{3,1,2,0:T(8,128)S(1)}, f32[8,64,6]{1,2,0:T(8,128)S(1)}, f32[32,8,64,6]{2,3,1,0:T(8,128)S(1)}, f32[8,64,64]{2,1,0:T(8...) while((s32[]{:T(128)}, f32[8,64,6,64]{3,1,2,0:T(8,128)S(1)}, ...), condition=%wide.region_1.2_spmd.clone, body=%wide.region_0.1_spmd.clone.sunk | while | flops 153560064 | bytes 3518595 | solution.py:70
  14.1 1.5 convolution_multiply_fusion.2
  16.9 1.5 convolution_multiply_fusion.2
  19.7 1.5 convolution_multiply_fusion.2
  22.6 1.5 convolution_multiply_fusion.2
  28.2 1.5 convolution_multiply_fusion.2
  31.0 1.5 convolution_multiply_fusion.2
  33.8 1.5 convolution_multiply_fusion.2
  36.6 1.5 convolution_multiply_fusion.2
  39.4 1.5 convolution_multiply_fusion.2
  42.2 1.5 convolution_multiply_fusion.2
  45.0 1.5 convolution_multiply_fusion.2
  47.8 1.5 convolution_multiply_fusion.2
  50.6 1.5 convolution_multiply_fusion.2
  53.5 1.5 convolution_multiply_fusion.2
  56.3 1.5 convolution_multiply_fusion.2
  59.1 1.5 convolution_multiply_fusion.2
  61.9 1.5 convolution_multiply_fusion.2
  64.7 1.5 convolution_multiply_fusion.2
  67.5 1.5 convolution_multiply_fusion.2
  70.3 1.5 convolution_multiply_fusion.2
  73.1 1.5 convolution_multiply_fusion.2
  78.7 1.5 convolution_multiply_fusion.2
  81.5 1.5 convolution_multiply_fusion.2
  84.3 1.5 convolution_multiply_fusion.2
  90.0 1.5 convolution_multiply_fusion.2
  95.6 1.5 convolution_multiply_fusion.2
  101.2 1.5 convolution_multiply_fusion.2
  108.0 1.6 copy.17
  111.3 1.8 convolution_bitcast_fusion.1
  113.1 8.5 %pad.66 = f32[8,64,5,64]{1,3,2,0:T(8,128)} pad(f32[8,64,3,64]{1,3,2,0:T(8,128)S(1)} %pad_add_fusion, f32[]{:T(128)} %constant.121.clone.1), padding=0_0_0x0_0_0x0_0_1x0_0_0 | pad | bytes 1048580
  121.6 8.6 %pad.33 = f32[8,64,6,64]{1,3,2,0:T(8,128)} pad(f32[8,64,3,64]{1,3,2,0:T(8,128)S(1)} %pad_add_fusion, f32[]{:T(128)} %constant.121.clone.1), padding=0_0_0x0_0_0x1_0_1x0_0_0 | pad | bytes 1179652 | tf_op jit(solution)/shard_map/pad | solution.py:74
  132.4 8.5 %pad.32 = f32[8,64,6,64]{1,3,2,0:T(8,128)} pad(f32[8,64,3,64]{1,3,2,0:T(8,128)S(1)} %pad_maximum_fusion, f32[]{:T(128)} %constant.121.clone.1), padding=0_0_0x0_0_0x0_1_1x0_0_0 | pad | bytes 1179652 | tf_op jit(solution)/shard_map/pad | solution.py:74
  142.7 47.1 %while.43 = (s32[]{:T(128)}, f32[8,64,1]{1,0,2:T(8,128)S(1)}, f32[8,64,1]{1,2,0:T(1,128)S(1)}, f32[8,64,1,64]{3,2,1,0:T(1,128)S(1)}, s32[]{:T(128)}) while((s32[]{:T(128)}, f32[8,64,1]{1,0,2:T(8,128)S(1)}, f32[8,64,1]{1,2,0:T(1,128)S(1)}, f32[8,64,1,64]{3,2,1,0:T(1,128)S(1)}, s32[]{:T(128)}) %tuple.90), condition=%wide.region_3.4_spmd, body=%wide.region_2.3_spmd.sunk | while | flops 393730 | bytes 149605 | solution.py:84
  144.6 4.2 %collective-permute-done = f32[8,64,1]{1,0,2:T(8,128)S(1)} collective-permute-done((f32[8,64,1]{1,0,2:T(8,128)S(1)}, f32[8,64,1]{1,0,2:T(8,128)S(1)}, u32[]{:S(2)}, u32[]{:S(2)}) %collective-permute-start) | collective-permute-done | bytes 2080 | tf_op jit(solution)/shard_map/while/body/eval_jaxpr/ppermute | solution.py:30
  150.6 4.6 %collective-permute-done = f32[8,64,1]{1,0,2:T(8,128)S(1)} collective-permute-done((f32[8,64,1]{1,0,2:T(8,128)S(1)}, f32[8,64,1]{1,0,2:T(8,128)S(1)}, u32[]{:S(2)}, u32[]{:S(2)}) %collective-permute-start) | collective-permute-done | bytes 2080 | tf_op jit(solution)/shard_map/while/body/eval_jaxpr/ppermute | solution.py:30
  157.0 5.1 %collective-permute-done = f32[8,64,1]{1,0,2:T(8,128)S(1)} collective-permute-done((f32[8,64,1]{1,0,2:T(8,128)S(1)}, f32[8,64,1]{1,0,2:T(8,128)S(1)}, u32[]{:S(2)}, u32[]{:S(2)}) %collective-permute-start) | collective-permute-done | bytes 2080 | tf_op jit(solution)/shard_map/while/body/eval_jaxpr/ppermute | solution.py:30
  163.9 5.1 %collective-permute-done = f32[8,64,1]{1,0,2:T(8,128)S(1)} collective-permute-done((f32[8,64,1]{1,0,2:T(8,128)S(1)}, f32[8,64,1]{1,0,2:T(8,128)S(1)}, u32[]{:S(2)}, u32[]{:S(2)}) %collective-permute-start) | collective-permute-done | bytes 2080 | tf_op jit(solution)/shard_map/while/body/eval_jaxpr/ppermute | solution.py:30
  170.8 5.1 %collective-permute-done = f32[8,64,1]{1,0,2:T(8,128)S(1)} collective-permute-done((f32[8,64,1]{1,0,2:T(8,128)S(1)}, f32[8,64,1]{1,0,2:T(8,128)S(1)}, u32[]{:S(2)}, u32[]{:S(2)}) %collective-permute-start) | collective-permute-done | bytes 2080 | tf_op jit(solution)/shard_map/while/body/eval_jaxpr/ppermute | solution.py:30
  177.8 5.1 %collective-permute-done = f32[8,64,1]{1,0,2:T(8,128)S(1)} collective-permute-done((f32[8,64,1]{1,0,2:T(8,128)S(1)}, f32[8,64,1]{1,0,2:T(8,128)S(1)}, u32[]{:S(2)}, u32[]{:S(2)}) %collective-permute-start) | collective-permute-done | bytes 2080 | tf_op jit(solution)/shard_map/while/body/eval_jaxpr/ppermute | solution.py:30
  184.7 5.1 %collective-permute-done = f32[8,64,1]{1,0,2:T(8,128)S(1)} collective-permute-done((f32[8,64,1]{1,0,2:T(8,128)S(1)}, f32[8,64,1]{1,0,2:T(8,128)S(1)}, u32[]{:S(2)}, u32[]{:S(2)}) %collective-permute-start) | collective-permute-done | bytes 2080 | tf_op jit(solution)/shard_map/while/body/eval_jaxpr/ppermute | solution.py:30
  189.8 2.2 fusion.24
  192.8 37.2 %while.44 = (s32[]{:T(128)}, f32[8,64,6]{1,2,0:T(8,128)S(1)}, bf16[32,8,64,6]{2,3,1,0:T(8,128)(2,1)S(1)}, f32[32,8,64,6]{2,3,1,0:T(8,128)}, f32[32,8,64,6]{2,3,1...) while((s32[]{:T(128)}, f32[8,64,6]{1,2,0:T(8,128)S(1)}, ...), condition=%wide.region_5.6_spmd, body=%wide.region_4.5_spmd.sunk | while | flops 2365443 | bytes 409701 | solution.py:99
  233.0 3.4 collective-permute-done.3
  236.4 2.7 fusion.25
  239.1 89.4 %reduce-scatter.2.cloned.1.call-done = f32[256,512]{1,0:T(8,128)} async-done(((f32[2048,512]{1,0:T(8,128)}), f32[256,512]{1,0:T(8,128)}) %reduce-scatter.2.cloned.1.call-update) | async-done | bytes 524304 | tf_op jit(solution)/shard_map/reduce_scatter | solution.py:106
  328.6 12.3 %all_to_all.19 = f32[4,64,512]{2,1,0:T(8,128)S(1)} all-to-all(f32[4,64,512]{2,1,0:T(8,128)} %bitcast.156), channel_id=1, replica_groups=mesh['ctx'=8,'tp'=4] {'tp'}, dimensions={0} | all-to-all | bytes 1048576 | tf_op jit(solution)/shard_map/all_to_all | solution.py:114
  (299 shorter events, 115.1 us)
Async XLA Ops:
  6.5 322.0 %reduce-scatter.2.cloned.1.call-start = ((), (), s32[]{:S(2)}) async-start(), calls=%async_computation.2 | async-start | bytes 4718592 | tf_op jit(solution)/shard_map/reduce_scatter | solution.py:106
  6.5 225.5 %collective-permute-start.2 = (bf16[192,512]{1,0:T(8,128)(2,1)}, bf16[192,512]{1,0:T(8,128)(2,1)}, u32[]{:S(2)}, u32[]{:S(2)}) collective-permute-start(bf16[192,512]{1,0:T(8,128)(2,1)} %param.10), channel_id=1, source_target_pairs={{0,3},{1,0},{2,1},{3,2},{4,7},{5,4},{6,5},{7,6},{8,11},{9,8},{10,9... | collective-permute-start | bytes 589832 | tf_op jit(solution)/shard_map/ppermute | solution.py:20
  8.9 222.1 %collective-permute-start.1 = (bf16[192,512]{1,0:T(8,128)(2,1)}, bf16[192,512]{1,0:T(8,128)(2,1)}, u32[]{:S(2)}, u32[]{:S(2)}) collective-permute-start(bf16[192,512]{1,0:T(8,128)(2,1)} %param.10), channel_id=1, source_target_pairs={{0,1},{1,2},{2,3},{3,0},{4,5},{5,6},{6,7},{7,4},{8,9},{9,10},{10,1... | collective-permute-start | bytes 589832 | tf_op jit(solution)/shard_map/ppermute | solution.py:17
  10.0 1.0 copy-start.4
  11.1 1.7 copy-start
  102.7 1.0 copy-start.3
  108.0 2.0 copy-start.2
  121.6 9.7 %slice-start = ((f32[8,64,6,64]{1,3,2,0:T(8,128)}), f32[8,64,1,64]{1,3,2,0:T(8,128)S(1)}, s32[]{:S(2)}) async-start(f32[8,64,6,64]{1,3,2,0:T(8,128)} %copy.17), calls=%async_computation.3 | async-start | bytes 524288 | tf_op jit(solution)/shard_map/slice | solution.py:74
  132.4 8.5 %slice-start.1 = ((f32[8,64,5,64]{1,3,2,0:T(8,128)}), f32[8,64,1,64]{1,3,2,0:T(8,128)S(1)}, s32[]{:S(2)}) async-start(f32[8,64,5,64]{1,3,2,0:T(8,128)} %pad.66), calls=%async_computation.4 | async-start | bytes 524288 | tf_op jit(solution)/shard_map/slice | solution.py:77
  132.4 8.7 %copy-start.1 = (f32[8,64,6,64]{1,3,2,0:T(8,128)S(1)}, f32[8,64,6,64]{1,3,2,0:T(8,128)}, u32[]{:S(2)}) copy-start(f32[8,64,6,64]{1,3,2,0:T(8,128)} %pad.33) | copy-start | bytes 2359300
  143.3 5.5 %collective-permute-start = (f32[8,64,1]{1,0,2:T(8,128)S(1)}, f32[8,64,1]{1,0,2:T(8,128)S(1)}, u32[]{:S(2)}, u32[]{:S(2)}) collective-permute-start(f32[8,64,1]{1,0,2:T(8,128)S(1)} %add_bitcast_fusion.2), channel_id=1, source_target_pairs={{4,0},{8,4},{12,8},{16,12},{20,16},{24,20},{28,24},{5,1},{9,5},{13... | collective-permute-start | bytes 6152 | tf_op jit(solution)/shard_map/while/body/eval_jaxpr/ppermute | solution.py:30
  149.3 5.9 %collective-permute-start = (f32[8,64,1]{1,0,2:T(8,128)S(1)}, f32[8,64,1]{1,0,2:T(8,128)S(1)}, u32[]{:S(2)}, u32[]{:S(2)}) collective-permute-start(f32[8,64,1]{1,0,2:T(8,128)S(1)} %add_bitcast_fusion.2), channel_id=1, source_target_pairs={{4,0},{8,4},{12,8},{16,12},{20,16},{24,20},{28,24},{5,1},{9,5},{13... | collective-permute-start | bytes 6152 | tf_op jit(solution)/shard_map/while/body/eval_jaxpr/ppermute | solution.py:30
  155.7 6.4 %collective-permute-start = (f32[8,64,1]{1,0,2:T(8,128)S(1)}, f32[8,64,1]{1,0,2:T(8,128)S(1)}, u32[]{:S(2)}, u32[]{:S(2)}) collective-permute-start(f32[8,64,1]{1,0,2:T(8,128)S(1)} %add_bitcast_fusion.2), channel_id=1, source_target_pairs={{4,0},{8,4},{12,8},{16,12},{20,16},{24,20},{28,24},{5,1},{9,5},{13... | collective-permute-start | bytes 6152 | tf_op jit(solution)/shard_map/while/body/eval_jaxpr/ppermute | solution.py:30
  162.6 6.4 %collective-permute-start = (f32[8,64,1]{1,0,2:T(8,128)S(1)}, f32[8,64,1]{1,0,2:T(8,128)S(1)}, u32[]{:S(2)}, u32[]{:S(2)}) collective-permute-start(f32[8,64,1]{1,0,2:T(8,128)S(1)} %add_bitcast_fusion.2), channel_id=1, source_target_pairs={{4,0},{8,4},{12,8},{16,12},{20,16},{24,20},{28,24},{5,1},{9,5},{13... | collective-permute-start | bytes 6152 | tf_op jit(solution)/shard_map/while/body/eval_jaxpr/ppermute | solution.py:30
  169.5 6.4 %collective-permute-start = (f32[8,64,1]{1,0,2:T(8,128)S(1)}, f32[8,64,1]{1,0,2:T(8,128)S(1)}, u32[]{:S(2)}, u32[]{:S(2)}) collective-permute-start(f32[8,64,1]{1,0,2:T(8,128)S(1)} %add_bitcast_fusion.2), channel_id=1, source_target_pairs={{4,0},{8,4},{12,8},{16,12},{20,16},{24,20},{28,24},{5,1},{9,5},{13... | collective-permute-start | bytes 6152 | tf_op jit(solution)/shard_map/while/body/eval_jaxpr/ppermute | solution.py:30
  176.5 6.4 %collective-permute-start = (f32[8,64,1]{1,0,2:T(8,128)S(1)}, f32[8,64,1]{1,0,2:T(8,128)S(1)}, u32[]{:S(2)}, u32[]{:S(2)}) collective-permute-start(f32[8,64,1]{1,0,2:T(8,128)S(1)} %add_bitcast_fusion.2), channel_id=1, source_target_pairs={{4,0},{8,4},{12,8},{16,12},{20,16},{24,20},{28,24},{5,1},{9,5},{13... | collective-permute-start | bytes 6152 | tf_op jit(solution)/shard_map/while/body/eval_jaxpr/ppermute | solution.py:30
  183.4 6.4 %collective-permute-start = (f32[8,64,1]{1,0,2:T(8,128)S(1)}, f32[8,64,1]{1,0,2:T(8,128)S(1)}, u32[]{:S(2)}, u32[]{:S(2)}) collective-permute-start(f32[8,64,1]{1,0,2:T(8,128)S(1)} %add_bitcast_fusion.2), channel_id=1, source_target_pairs={{4,0},{8,4},{12,8},{16,12},{20,16},{24,20},{28,24},{5,1},{9,5},{13... | collective-permute-start | bytes 6152 | tf_op jit(solution)/shard_map/while/body/eval_jaxpr/ppermute | solution.py:30
  230.1 0.9 copy-start.5
  231.0 5.4 %collective-permute-start.3 = (bf16[192,512]{1,0:T(8,128)(2,1)}, bf16[192,512]{1,0:T(8,128)(2,1)S(1)}, u32[]{:S(2)}, u32[]{:S(2)}) collective-permute-start(bf16[192,512]{1,0:T(8,128)(2,1)} %collective-permute-done.1), channel_id=1, source_target_pairs={{0,1},{1,2},{2,3},{3,0},{4,5},{5,6},{6,7},{7,4},{8,9},{9,10},{10,1... | collective-permute-start | bytes 589832 | tf_op jit(solution)/shard_map/ppermute | solution.py:17
Sparse Core Ops, SparseCore 0:
  239.3 89.2 reduce-scatter.1
